TPU v7x, 256 devices: a whole 4x4x8 slice. The times are simulated.
256 devices in a mesh: seq: 8 (over x_hi, y), row: 32 (over x_lo, z, core).
Axes of the slice: x: 4 (x_hi: 2, x_lo: 2; x = x_hi * 2 + x_lo), y: 4, z: 8, core: 2. Of those that a mesh axis runs over, the one named last changes fastest.
Arguments:
- tokens: bfloat16 [2, 2048, 3072], P(None, ('seq', 'row')), may hold values from -6 to 6
- w_qkv: bfloat16 [6144, 3072], P('row'), may hold values from -0.109375 to 0.109375
- w_rate: bfloat16 [32, 3072], P('row'), may hold values from -0.109375 to 0.109375
- rate_bias: float32 [32], P('row'), may hold values from -3 to 1
- w_out: bfloat16 [2048, 3072], P('row'), may hold values from -0.125 to 0.125
- w_first_init: float32 [32, 64, 256], P('row'), may hold values from -0.75 to 0.75
- b_first_init: float32 [32, 256], P('row'), may hold values from -3 to 3
- w_second_init: float32 [32, 256, 64], P('row'), may hold values from -0.375 to 0.375
- b_second_init: float32 [32, 64], P('row'), may hold values from -3 to 3
- ln_gain: float32 [32, 64], P('row'), may hold values from 0.5 to 1.5
- ln_bias: float32 [32, 64], P('row'), may hold values from -3 to 3
Outputs:
- mixed: bfloat16 [2, 2048, 3072], P(None, ('seq', 'row'))
All inputs are finite; a program needn't handle non-finite values.
Results may differ from a plain program's by a relative error of at most 0.0056.
Values may be sent and summed in bfloat16 or wider, within the bound.
A program may use at most 64 MiB of HBM per device.

v0:
```python
from functools import partial
import jax
import jax.numpy as jnp
from jax import lax
from jax.sharding import PartitionSpec as P

MINI = 64
gelu_coef = 0.7978845608028654
base_rate = 0.01
ln_eps = 1e-06


def passed_along(array, axis, by):
    size = lax.axis_size(axis)
    pairs = [(i, i + by) for i in range(size) if 0 <= i + by < size]
    return lax.ppermute(array, axis, pairs)


def gelu_tanh(entries):
    tanh_arg = gelu_coef * (entries + 0.044715 * entries * entries * entries)
    return 0.5 * entries * (1.0 + jnp.tanh(tanh_arg))


def gelu_slope(entries):
    tanh_arg = gelu_coef * (entries + 0.044715 * entries * entries * entries)
    tangent = jnp.tanh(tanh_arg)
    return 0.5 * (1.0 + tangent) + 0.5 * entries * (1.0 - tangent * tangent) * gelu_coef * (
        1.0 + 3.0 * 0.044715 * entries * entries
    )


def matmul(left, right):
    return jnp.dot(left, right, precision=lax.Precision.HIGHEST, preferred_element_type=jnp.float32)


def normalize(entries):
    centred = entries - jnp.mean(entries, axis=-1, keepdims=True)
    spread = jnp.sqrt(jnp.mean(centred * centred, axis=-1, keepdims=True) + ln_eps)
    return (centred / spread, spread)


def mini_step(inner_state, batch_block, norm_gain, offset):
    w_first, b_first, w_second, b_second = inner_state
    queries, key_rows, value_rows, lr_rows = batch_block
    mini_len = queries.shape[0]
    hidden_pre = matmul(key_rows, w_first) + b_first
    hidden = gelu_tanh(hidden_pre)
    second = matmul(hidden, w_second) + b_second
    target = value_rows - key_rows
    normed, spread = normalize(second)
    grad_out = norm_gain * (norm_gain * normed + offset - target)
    feat_width = second.shape[-1]
    grad_second = (
        feat_width * grad_out
        - jnp.sum(grad_out, axis=-1, keepdims=True)
        - normed * jnp.sum(grad_out * normed, axis=-1, keepdims=True)
    ) / (feat_width * spread)
    grad_first = matmul(grad_second, w_second.T) * gelu_slope(hidden_pre)
    tri_mask = jnp.tril(jnp.ones((mini_len, mini_len), jnp.float32))
    eta_last = lr_rows / mini_len
    eta_table = tri_mask * eta_last[None, :]
    query_keys = matmul(queries, key_rows.T) * eta_table
    bias_first = b_first - matmul(eta_table, grad_first)
    first_bar = matmul(queries, w_first) - matmul(query_keys, grad_first) + bias_first
    hidden_bar = gelu_tanh(first_bar)
    hidden_pairs = matmul(hidden_bar, hidden.T) * eta_table
    bias_second = b_second - matmul(eta_table, grad_second)
    second_bar = matmul(hidden_bar, w_second) - matmul(hidden_pairs, grad_second) + bias_second
    w_first = w_first - matmul((key_rows * eta_last[:, None]).T, grad_first)
    b_first = b_first - matmul(eta_last[None, :], grad_first)[0]
    w_second = w_second - matmul((hidden * eta_last[:, None]).T, grad_second)
    b_second = b_second - matmul(eta_last[None, :], grad_second)[0]
    normed_bar, spread_bar = normalize(second_bar)
    result = queries + norm_gain * normed_bar + offset
    return ((w_first, b_first, w_second, b_second), result)


def run_blocks(inner_state, queries, key_rows, value_rows, lr_rows, norm_gain, offset, mini_len):
    block_count = queries.shape[0] // mini_len
    blocks = (
        queries.reshape(block_count, mini_len, -1),
        key_rows.reshape(block_count, mini_len, -1),
        value_rows.reshape(block_count, mini_len, -1),
        lr_rows.reshape(block_count, mini_len),
    )

    def advance(loop_carry, batch_block):
        return mini_step(loop_carry, batch_block, norm_gain, offset)

    inner_state, results = lax.scan(advance, inner_state, blocks)
    return (inner_state, results.reshape(queries.shape[0], -1))


def pack_state(state):
    videos = state[0].shape[0]
    return jnp.concatenate([part.reshape(videos, -1) for part in state], axis=1)


def unpack_state(flat, like):
    parts = []
    at = 0
    for part in like:
        width = part[0].size
        parts.append(flat[:, at : at + width].reshape(part.shape))
        at += width
    return tuple(parts)


def on_device(
    tokens,
    w_qkv,
    w_rate,
    rate_bias,
    w_out,
    w_first_init,
    b_first_init,
    w_second_init,
    b_second_init,
    ln_gain,
    ln_bias,
):
    videos, tok_part, feat_width = tokens.shape
    row_axes = ("xlo", "z", "core")
    pair_axes = ("xlo", "core")
    row_count = lax.axis_size(row_axes)
    z_count = lax.axis_size("z")
    pair_count = lax.axis_size(pair_axes)
    seg_len = tok_part * row_count
    proj_width = w_qkv.shape[0]
    head_size = proj_width // 3
    stacked = jnp.concatenate([w_qkv, w_rate], axis=0)
    gathered = lax.all_gather(tokens, row_axes, axis=1, tiled=True)
    gathered, w_out = lax.optimization_barrier((gathered, w_out))
    w_out_pair = lax.all_gather(w_out, pair_axes, axis=0, tiled=True)
    combined = jnp.einsum("vkd,cd->vkc", gathered, stacked, preferred_element_type=jnp.float32)
    projected = lax.optimization_barrier(combined[:, :, :proj_width].astype(jnp.bfloat16)).astype(
        jnp.float32
    )
    queries = projected[:, :, :head_size]
    key_rows = projected[:, :, head_size : 2 * head_size]
    value_rows = projected[:, :, 2 * head_size :]
    lr_rows = base_rate * jax.nn.sigmoid(combined[:, :, proj_width] + rate_bias[0])
    initial = (w_first_init[0], b_first_init[0], w_second_init[0], b_second_init[0])
    norm_gain = ln_gain[0]
    offset = ln_bias[0]

    def segment(inner_state, video_q, video_k, video_v, video_lr):
        return run_blocks(inner_state, video_q, video_k, video_v, video_lr, norm_gain, offset, MINI)

    seq_count = lax.axis_size("seq")
    seq_place = lax.axis_index("seq")
    first_device = seq_place == 0

    def spread_videos(entries):
        return jnp.broadcast_to(entries, (videos,) + entries.shape)

    start_states = jax.tree.map(spread_videos, initial)
    incoming = start_states
    for turn_idx in range(seq_count):
        finals, results = jax.vmap(segment)(incoming, queries, key_rows, value_rows, lr_rows)
        if turn_idx + 1 < seq_count:
            with jax.named_scope("state_hop"):
                received = unpack_state(passed_along(pack_state(finals), "seq", 1), finals)
            incoming = jax.tree.map(partial(jnp.where, first_device), start_states, received)
    heads_rows = results.astype(jnp.bfloat16)
    with jax.named_scope("output_mix"):
        by_owner = heads_rows.reshape(videos, 2, z_count, 2, tok_part, head_size)
        by_owner = by_owner.transpose(1, 3, 0, 2, 4, 5).reshape(
            pair_count, videos, z_count, tok_part, head_size
        )
        by_head = lax.all_to_all(by_owner, pair_axes, 0, 0, tiled=True)
        partial_terms = jnp.einsum(
            "gvzic,gcd->zvid",
            by_head,
            w_out_pair.reshape(pair_count, head_size, feat_width),
            preferred_element_type=jnp.float32,
        )
        mixed_out = lax.psum_scatter(
            partial_terms.reshape(z_count, -1), "z", scatter_dimension=0, tiled=True
        )
        mixed_out = lax.optimization_barrier(mixed_out)
    return mixed_out.reshape(videos, tok_part, feat_width).astype(jnp.bfloat16)


def solution(mesh):
    seq_count, row_count = mesh.devices.shape
    fine = jax.sharding.Mesh(
        mesh.devices.reshape(seq_count, 2, row_count // 4, 2), ("seq", "xlo", "z", "core")
    )
    row = ("xlo", "z", "core")
    in_specs = (
        P(None, ("seq",) + row, None),
        P(row, None),
        P(row, None),
        P(row),
        P(row, None),
        P(row, None, None),
        P(row, None),
        P(row, None, None),
        P(row, None),
        P(row, None),
        P(row, None),
    )
    out_specs = P(None, ("seq",) + row, None)
    return jax.shard_map(
        on_device, mesh=fine, in_specs=in_specs, out_specs=out_specs, check_vma=False
    )
```

profile of v0, /device:TPU:4, one launch (start us, length us, event | category | flops | bytes accessed | tf_op | source)
XLA Modules:
  0.0 355.5 jit_solution(17340669928445101169)
XLA Ops:
  6.5 0.7 all-gather.3.cloned.1.call-update
  7.9 70.0 %all-gather.3.cloned.1.call-done = bf16[2,256,3072]{2,1,0:T(8,128)(2,1)} async-done(((bf16[2,8,3072]{2,1,0:T(8,128)(2,1)}), bf16[2,256,3072]{2,1,0:T(8,128)(2,1)}) %all-gather.3.cloned.1.call-update) | async-done | bytes 3145744 | tf_op jit(solution)/shard_map/all_gather | solution.py:132
  78.0 3.4 fusion.200
  82.3 10.8 %while.130 = (s32[]{:T(128)}, f32[2,64,256]{2,1,0:T(8,128)S(1)}, f32[2,256]{1,0:T(2,128)S(1)}, f32[2,256,64]{1,2,0:T(8,128)S(1)}, f32[2,64]{1,0:T(2,128)S(1)}, /...) while((s32[]{:T(128)}, f32[2,64,256]{2,1,0:T(8,128)S(1)}, ...), condition=%wide.region_5.6_spmd, body=%wide.region_0.5_spmd.sunk | while | flops 127755136 | bytes 2386049 | solution.py:90
  93.7 3.4 collective-permute-start
  97.2 10.5 %collective-permute-done = f32[2,33088]{1,0:T(2,128)S(1)} collective-permute-done((f32[2,33088]{1,0:T(2,128)S(1)}, f32[2,33088]{1,0:T(2,128)S(1)}, u32[]{:S(2)}, u32[]{:S(2)}) %collective-permute-start) | collective-permute-done | bytes 264736 | tf_op jit(solution)/shard_map/state_hop/ppermute | solution.py:16
  108.1 10.8 %while.131 = (s32[]{:T(128)}, f32[2,64,256]{2,1,0:T(8,128)S(1)}, f32[2,256]{1,0:T(2,128)S(1)}, f32[2,256,64]{1,2,0:T(8,128)S(1)}, f32[2,64]{1,0:T(2,128)S(1)}, /...) while((s32[]{:T(128)}, f32[2,64,256]{2,1,0:T(8,128)S(1)}, ...), condition=%wide.region_11.12_spmd, body=%wide.region_6.11_spmd.sunk | while | flops 127755136 | bytes 2386049 | solution.py:90
  112.7 0.4 convolution_subtract_fusion.40
  118.1 0.4 convolution_subtract_fusion.40
  119.5 1.9 collective-permute-start.1
  121.4 11.3 %collective-permute-done.1 = f32[2,33088]{1,0:T(2,128)S(1)} collective-permute-done((f32[2,33088]{1,0:T(2,128)S(1)}, f32[2,33088]{1,0:T(2,128)S(1)}, u32[]{:S(2)}, u32[]{:S(2)}) %collective-permute-start.1) | collective-permute-done | bytes 264736 | tf_op jit(solution)/shard_map/state_hop/ppermute | solution.py:16
  133.1 10.8 %while.132 = (s32[]{:T(128)}, f32[2,64,256]{2,1,0:T(8,128)S(1)}, f32[2,256]{1,0:T(2,128)S(1)}, f32[2,256,64]{1,2,0:T(8,128)S(1)}, f32[2,64]{1,0:T(2,128)S(1)}, /...) while((s32[]{:T(128)}, f32[2,64,256]{2,1,0:T(8,128)S(1)}, ...), condition=%wide.region_17.18_spmd, body=%wide.region_12.17_spmd.sunk | while | flops 127755136 | bytes 2386049 | solution.py:90
  137.7 0.4 convolution_subtract_fusion.42
  143.1 0.4 convolution_subtract_fusion.42
  144.4 1.9 collective-permute-start.2
  146.4 10.4 %collective-permute-done.2 = f32[2,33088]{1,0:T(2,128)S(1)} collective-permute-done((f32[2,33088]{1,0:T(2,128)S(1)}, f32[2,33088]{1,0:T(2,128)S(1)}, u32[]{:S(2)}, u32[]{:S(2)}) %collective-permute-start.2) | collective-permute-done | bytes 264736 | tf_op jit(solution)/shard_map/state_hop/ppermute | solution.py:16
  157.1 10.8 %while.133 = (s32[]{:T(128)}, f32[2,64,256]{2,1,0:T(8,128)S(1)}, f32[2,256]{1,0:T(2,128)S(1)}, f32[2,256,64]{1,2,0:T(8,128)S(1)}, f32[2,64]{1,0:T(2,128)S(1)}, /...) while((s32[]{:T(128)}, f32[2,64,256]{2,1,0:T(8,128)S(1)}, ...), condition=%wide.region_23.24_spmd, body=%wide.region_18.23_spmd.sunk | while | flops 127755136 | bytes 2386049 | solution.py:90
  161.7 0.4 convolution_subtract_fusion.44
  167.2 0.4 convolution_subtract_fusion.44
  168.5 2.1 collective-permute-start.3
  170.6 9.8 %collective-permute-done.3 = f32[2,33088]{1,0:T(2,128)S(1)} collective-permute-done((f32[2,33088]{1,0:T(2,128)S(1)}, f32[2,33088]{1,0:T(2,128)S(1)}, u32[]{:S(2)}, u32[]{:S(2)}) %collective-permute-start.3) | collective-permute-done | bytes 264736 | tf_op jit(solution)/shard_map/state_hop/ppermute | solution.py:16
  180.8 10.8 %while.134 = (s32[]{:T(128)}, f32[2,64,256]{2,1,0:T(8,128)S(1)}, f32[2,256]{1,0:T(2,128)S(1)}, f32[2,256,64]{1,2,0:T(8,128)S(1)}, f32[2,64]{1,0:T(2,128)S(1)}, /...) while((s32[]{:T(128)}, f32[2,64,256]{2,1,0:T(8,128)S(1)}, ...), condition=%wide.region_29.30_spmd, body=%wide.region_24.29_spmd.sunk | while | flops 127755136 | bytes 2386049 | solution.py:90
  185.4 0.4 convolution_subtract_fusion.46
  190.8 0.4 convolution_subtract_fusion.46
  192.2 1.9 collective-permute-start.4
  194.1 10.0 %collective-permute-done.4 = f32[2,33088]{1,0:T(2,128)S(1)} collective-permute-done((f32[2,33088]{1,0:T(2,128)S(1)}, f32[2,33088]{1,0:T(2,128)S(1)}, u32[]{:S(2)}, u32[]{:S(2)}) %collective-permute-start.4) | collective-permute-done | bytes 264736 | tf_op jit(solution)/shard_map/state_hop/ppermute | solution.py:16
  204.5 10.8 %while.135 = (s32[]{:T(128)}, f32[2,64,256]{2,1,0:T(8,128)S(1)}, f32[2,256]{1,0:T(2,128)S(1)}, f32[2,256,64]{1,2,0:T(8,128)S(1)}, f32[2,64]{1,0:T(2,128)S(1)}, /...) while((s32[]{:T(128)}, f32[2,64,256]{2,1,0:T(8,128)S(1)}, ...), condition=%wide.region_35.36_spmd, body=%wide.region_30.35_spmd.sunk | while | flops 127755136 | bytes 2386049 | solution.py:90
  209.1 0.4 convolution_subtract_fusion.48
  214.5 0.4 convolution_subtract_fusion.48
  215.8 1.9 collective-permute-start.5
  217.8 10.0 %collective-permute-done.5 = f32[2,33088]{1,0:T(2,128)S(1)} collective-permute-done((f32[2,33088]{1,0:T(2,128)S(1)}, f32[2,33088]{1,0:T(2,128)S(1)}, u32[]{:S(2)}, u32[]{:S(2)}) %collective-permute-start.5) | collective-permute-done | bytes 264736 | tf_op jit(solution)/shard_map/state_hop/ppermute | solution.py:16
  228.2 10.8 %while.136 = (s32[]{:T(128)}, f32[2,64,256]{2,1,0:T(8,128)S(1)}, f32[2,256]{1,0:T(2,128)S(1)}, f32[2,256,64]{1,2,0:T(8,128)S(1)}, f32[2,64]{1,0:T(2,128)S(1)}, /...) while((s32[]{:T(128)}, f32[2,64,256]{2,1,0:T(8,128)S(1)}, ...), condition=%wide.region_41.42_spmd, body=%wide.region_36.41_spmd.sunk | while | flops 127755136 | bytes 2386049 | solution.py:90
  232.8 0.4 convolution_subtract_fusion.50
  238.2 0.4 convolution_subtract_fusion.50
  239.5 1.9 collective-permute-start.6
  241.8 9.6 %collective-permute-done.6 = f32[2,33088]{1,0:T(2,128)S(1)} collective-permute-done((f32[2,33088]{1,0:T(2,128)S(1)}, f32[2,33088]{1,0:T(2,128)S(1)}, u32[]{:S(2)}, u32[]{:S(2)}) %collective-permute-start.6) | collective-permute-done | bytes 264736 | tf_op jit(solution)/shard_map/state_hop/ppermute | solution.py:16
  251.9 20.8 %while.137 = (s32[]{:T(128)}, f32[2,64,256]{2,1,0:T(8,128)S(1)}, f32[2,256]{1,0:T(2,128)S(1)}, f32[2,256,64]{1,2,0:T(8,128)S(1)}, f32[2,64]{1,0:T(2,128)S(1)}, /...) while((s32[]{:T(128)}, f32[2,64,256]{2,1,0:T(8,128)S(1)}, ...), condition=%wide.region_49.50_spmd, body=%wide.region_42.49_spmd.sunk | while | flops 273236992 | bytes 4856473 | solution.py:90
  261.5 0.4 convolution_subtract_fusion.52
  272.7 0.8 reshape.533
  273.5 3.5 all-to-all-start
  277.0 0.6 dynamic-slice
  277.6 3.2 all-to-all-done
  281.0 1.8 convolution_bitcast_fusion
  283.0 0.9 copy.288
  283.9 62.7 %all-reduce.2 = bf16[8,49152]{1,0:T(8,128)(2,1)S(1)} all-reduce(f32[8,49152]{1,0:T(8,128)S(1)} %bitcast.719), channel_id=2, replica_groups=mesh['seq'=8,'xlo'=2,'z'=8,'core'=2] {'z'}, use_global_device_ids=true, to_apply=%region_50.51.clone | all-reduce | flops 393216 | bytes 2359296
  346.6 0.8 constant_dynamic-slice_fusion.1
  347.5 0.6 convert_reduce_fusion
  348.0 0.7 convert_element_type.25
  (666 shorter events, 96.4 us)
Async XLA Ops:
  6.5 71.4 %all-gather.3.cloned.1.call-start = ((), (), s32[]{:S(2)}) async-start(), calls=%async_computation.1 | async-start | bytes 3244032 | tf_op jit(solution)/shard_map/all_gather | solution.py:132
  7.3 273.8 %all-gather.5.cloned.1.call-start = ((), (), s32[]{:S(2)}) async-start(), calls=%async_computation.2 | async-start | bytes 1966080 | tf_op jit(solution)/shard_map/all_gather | solution.py:134
  81.4 0.9 copy-start
  81.4 0.9 copy-start.4
  81.4 0.9 copy-start.5
  81.4 0.9 copy-start.3
  81.4 0.9 copy-start.1
  81.4 0.9 copy-start.2
  93.7 14.0 %collective-permute-start = (f32[2,33088]{1,0:T(2,128)S(1)}, f32[2,33088]{1,0:T(2,128)S(1)}, u32[]{:S(2)}, u32[]{:S(2)}) collective-permute-start(f32[2,33088]{1,0:T(2,128)S(1)} %pad_maximum_fusion), channel_id=1, source_target_pairs={{0,32},{32,64},{64,96},{96,128},{128,160},{160,192},{192,224},{1,3... | collective-permute-start | bytes 794120 | tf_op jit(solution)/shard_map/state_hop/ppermute | solution.py:16
  119.5 13.2 %collective-permute-start.1 = (f32[2,33088]{1,0:T(2,128)S(1)}, f32[2,33088]{1,0:T(2,128)S(1)}, u32[]{:S(2)}, u32[]{:S(2)}) collective-permute-start(f32[2,33088]{1,0:T(2,128)S(1)} %pad_maximum_fusion.1), channel_id=1, source_target_pairs={{0,32},{32,64},{64,96},{96,128},{128,160},{160,192},{192,224},{1,3... | collective-permute-start | bytes 794120 | tf_op jit(solution)/shard_map/state_hop/ppermute | solution.py:16
  144.4 12.3 %collective-permute-start.2 = (f32[2,33088]{1,0:T(2,128)S(1)}, f32[2,33088]{1,0:T(2,128)S(1)}, u32[]{:S(2)}, u32[]{:S(2)}) collective-permute-start(f32[2,33088]{1,0:T(2,128)S(1)} %pad_maximum_fusion.2), channel_id=1, source_target_pairs={{0,32},{32,64},{64,96},{96,128},{128,160},{160,192},{192,224},{1,3... | collective-permute-start | bytes 794120 | tf_op jit(solution)/shard_map/state_hop/ppermute | solution.py:16
  168.5 11.9 %collective-permute-start.3 = (f32[2,33088]{1,0:T(2,128)S(1)}, f32[2,33088]{1,0:T(2,128)S(1)}, u32[]{:S(2)}, u32[]{:S(2)}) collective-permute-start(f32[2,33088]{1,0:T(2,128)S(1)} %pad_maximum_fusion.3), channel_id=1, source_target_pairs={{0,32},{32,64},{64,96},{96,128},{128,160},{160,192},{192,224},{1,3... | collective-permute-start | bytes 794120 | tf_op jit(solution)/shard_map/state_hop/ppermute | solution.py:16
  192.2 11.9 %collective-permute-start.4 = (f32[2,33088]{1,0:T(2,128)S(1)}, f32[2,33088]{1,0:T(2,128)S(1)}, u32[]{:S(2)}, u32[]{:S(2)}) collective-permute-start(f32[2,33088]{1,0:T(2,128)S(1)} %pad_maximum_fusion.4), channel_id=1, source_target_pairs={{0,32},{32,64},{64,96},{96,128},{128,160},{160,192},{192,224},{1,3... | collective-permute-start | bytes 794120 | tf_op jit(solution)/shard_map/state_hop/ppermute | solution.py:16
  215.8 11.9 %collective-permute-start.5 = (f32[2,33088]{1,0:T(2,128)S(1)}, f32[2,33088]{1,0:T(2,128)S(1)}, u32[]{:S(2)}, u32[]{:S(2)}) collective-permute-start(f32[2,33088]{1,0:T(2,128)S(1)} %pad_maximum_fusion.5), channel_id=1, source_target_pairs={{0,32},{32,64},{64,96},{96,128},{128,160},{160,192},{192,224},{1,3... | collective-permute-start | bytes 794120 | tf_op jit(solution)/shard_map/state_hop/ppermute | solution.py:16
  239.5 11.9 %collective-permute-start.6 = (f32[2,33088]{1,0:T(2,128)S(1)}, f32[2,33088]{1,0:T(2,128)S(1)}, u32[]{:S(2)}, u32[]{:S(2)}) collective-permute-start(f32[2,33088]{1,0:T(2,128)S(1)} %pad_maximum_fusion.6), channel_id=1, source_target_pairs={{0,32},{32,64},{64,96},{96,128},{128,160},{160,192},{192,224},{1,3... | collective-permute-start | bytes 794120 | tf_op jit(solution)/shard_map/state_hop/ppermute | solution.py:16
  251.9 25.1 %copy-start.6 = (u32[256]{0:T(256)S(1)}, u32[256]{0:T(256)}, u32[]{:S(2)}) copy-start(u32[256]{0:T(256)} %constant.275) | copy-start | bytes 3076
  273.5 7.4 %all-to-all-start = ((bf16[4,2,4096]{2,1,0:T(2,128)(2,1)}), bf16[4,2,4096]{2,1,0:T(2,128)(2,1)S(1)}, u32[]{:S(2)}, u32[]{:S(2)}) async-start(bf16[4,2,4096]{2,1,0:T(2,128)(2,1)} %reshape.533), calls=%async_computation | async-start | bytes 131072 | tf_op jit(solution)/shard_map/output_mix/all_to_all | solution.py:171
Sparse Core Ops, SparseCore 0:
  9.2 68.7 all-gather.2
  241.9 27.2 all-gather.4
where the time goes:
time: 356 us
  waiting for transfers between devices  146 us (41%)
  matrix products  78.5 us (22%)
  blocking collectives  62.7 us (18%)
  other arithmetic  21.7 us (6%)
  starting transfers between devices  18.6 us (5%)
  between operations  14.9 us (4%)
  local copies, waits for them, and re-layouts  10.9 us (3%)
    dot_general x256, matrix products, matmul(): jnp.dot(left, right, precision=lax.Precision.HIGHEST, preferred_element_t...  73.3 us
    ppermute x7, waiting for transfers between devices, passed_along(): return lax.ppermute(array, axis, pairs)  71.6 us
    all_gather x1, waiting for transfers between devices, on_device(): gathered = lax.all_gather(tokens, row_axes, axis=1, tiled=True)  70 us
    unnamed x1, blocking collectives  62.7 us
    ppermute x7, starting transfers between devices, passed_along(): return lax.ppermute(array, axis, pairs)  15.1 us
  transfers between devices with their start and end apart: 10, of which 9 were waited for; matrix products, arithmetic and copies ran while one was open for 6% of the time, Pallas kernels for 0%

commit v1 on v0

--- a/solution.py
+++ b/solution.py
@@ -129,7 +129,17 @@
     proj_width = w_qkv.shape[0]
     head_size = proj_width // 3
     stacked = jnp.concatenate([w_qkv, w_rate], axis=0)
-    gathered = lax.all_gather(tokens, row_axes, axis=1, tiled=True)
+
+    def press_vector(block_here):
+        q_next = jnp.concatenate(
+            jax.lax.all_to_all(
+                jnp.stack(jax.lax.axis_size(row_axes) * [block_here], axis=0), row_axes, 0, 0
+            ),
+            axis=1,
+        )
+        return q_next
+
+    gathered = press_vector(tokens)
     gathered, w_out = lax.optimization_barrier((gathered, w_out))
     w_out_pair = lax.all_gather(w_out, pair_axes, axis=0, tiled=True)
     combined = jnp.einsum("vkd,cd->vkc", gathered, stacked, preferred_element_type=jnp.float32)

time: 356 us -> 368 us (1.034)
  starting transfers between devices: 18.6 us -> 28.2 us
  local copies, waits for them, and re-layouts: 10.9 us -> 15.1 us
    all_to_all x0 -> x1, waiting for transfers between devices: none -> 72.1 us  [press_vector(): jax.lax.all_to_all(jnp.stack(jax.lax.axis_size(row_axes) * [block_here],...]
    all_gather x1 -> x0, waiting for transfers between devices: 70 us -> none  [on_device(): gathered = lax.all_gather(tokens, row_axes, axis=1, tiled=True)]
    all_to_all x0 -> x1, starting transfers between devices: none -> 9.49 us  [press_vector(): jax.lax.all_to_all(jnp.stack(jax.lax.axis_size(row_axes) * [block_here],...]
where the time goes in v1:
time: 368 us; the launch traced here: 367 us
  waiting for transfers between devices  145 us (39%)
  matrix products  76.3 us (21%)
  blocking collectives  63.4 us (17%)
  starting transfers between devices  28.2 us (8%)
  other arithmetic  21.7 us (6%)
  local copies, waits for them, and re-layouts  15.1 us (4%)
  between operations  14.9 us (4%)
    dot_general x256, matrix products, matmul(): jnp.dot(left, right, precision=lax.Precision.HIGHEST, preferred_element_t...  73.3 us
    all_to_all x1, waiting for transfers between devices, press_vector(): jax.lax.all_to_all(jnp.stack(jax.lax.axis_size(row_axes) * [block_here],...  72.1 us
    ppermute x7, waiting for transfers between devices, passed_along(): return lax.ppermute(array, axis, pairs)  69.5 us
    unnamed x1, blocking collectives  63.4 us
    ppermute x7, starting transfers between devices, passed_along(): return lax.ppermute(array, axis, pairs)  15.4 us
    all_to_all x1, starting transfers between devices, press_vector(): jax.lax.all_to_all(jnp.stack(jax.lax.axis_size(row_axes) * [block_here],...  9.49 us
  transfers between devices with their start and end apart: 10, of which 9 were waited for; matrix products, arithmetic and copies ran while one was open for 6% of the time, Pallas kernels for 0%

profile of v1, /device:TPU:4, one launch (start us, length us, event | category | flops | bytes accessed | tf_op | source)
XLA Modules:
  0.0 367.3 jit_solution(11450182284471782767)
XLA Ops:
  6.5 2.9 stack.2
  9.5 9.5 %all-to-all-start = ((bf16[32,2,8,3072]{3,2,1,0:T(8,128)(2,1)}), bf16[32,2,8,3072]{3,2,1,0:T(8,128)(2,1)S(1)}, u32[]{:S(2)}, u32[]{:S(2)}) async-start(bf16[32,2,8,3072]{3,2,1,0:T(8,128)(2,1)} %stack.2), calls=%async_computation | async-start | bytes 6291456 | tf_op jit(solution)/shard_map/all_to_all | solution.py:135
  19.7 72.1 %all-to-all-done = bf16[32,2,8,3072]{3,2,1,0:T(8,128)(2,1)S(1)} async-done(((bf16[32,2,8,3072]{3,2,1,0:T(8,128)(2,1)}), bf16[32,2,8,3072]{3,2,1,0:T(8,128)(2,1)S(1)}, u32[]{:S(2)}, u32[]{:S(2)}) %all-to-all-start) | async-done | bytes 3145760 | tf_op jit(solution)/shard_map/all_to_all | solution.py:135
  92.0 1.0 copy-done.6
  93.0 1.2 fusion.200
  95.2 10.8 %while.130 = (s32[]{:T(128)}, f32[2,64,256]{2,1,0:T(8,128)S(1)}, f32[2,256]{1,0:T(2,128)S(1)}, f32[2,256,64]{1,2,0:T(8,128)S(1)}, f32[2,64]{1,0:T(2,128)S(1)}, /...) while((s32[]{:T(128)}, f32[2,64,256]{2,1,0:T(8,128)S(1)}, ...), condition=%wide.region_5.6_spmd, body=%wide.region_0.5_spmd.sunk | while | flops 127755136 | bytes 2386049 | solution.py:90
  97.1 0.4 convolution_subtract_fusion.38
  102.5 0.4 convolution_subtract_fusion.38
  106.5 3.5 collective-permute-start
  110.1 9.8 %collective-permute-done = f32[2,33088]{1,0:T(2,128)S(1)} collective-permute-done((f32[2,33088]{1,0:T(2,128)S(1)}, f32[2,33088]{1,0:T(2,128)S(1)}, u32[]{:S(2)}, u32[]{:S(2)}) %collective-permute-start) | collective-permute-done | bytes 264736 | tf_op jit(solution)/shard_map/state_hop/ppermute | solution.py:16
  120.3 10.8 %while.131 = (s32[]{:T(128)}, f32[2,64,256]{2,1,0:T(8,128)S(1)}, f32[2,256]{1,0:T(2,128)S(1)}, f32[2,256,64]{1,2,0:T(8,128)S(1)}, f32[2,64]{1,0:T(2,128)S(1)}, /...) while((s32[]{:T(128)}, f32[2,64,256]{2,1,0:T(8,128)S(1)}, ...), condition=%wide.region_11.12_spmd, body=%wide.region_6.11_spmd.sunk | while | flops 127755136 | bytes 2386049 | solution.py:90
  127.6 0.4 convolution_subtract_fusion.40
  130.3 0.4 convolution_subtract_fusion.40
  131.7 1.9 collective-permute-start.1
  133.6 10.5 %collective-permute-done.1 = f32[2,33088]{1,0:T(2,128)S(1)} collective-permute-done((f32[2,33088]{1,0:T(2,128)S(1)}, f32[2,33088]{1,0:T(2,128)S(1)}, u32[]{:S(2)}, u32[]{:S(2)}) %collective-permute-start.1) | collective-permute-done | bytes 264736 | tf_op jit(solution)/shard_map/state_hop/ppermute | solution.py:16
  144.6 10.8 %while.132 = (s32[]{:T(128)}, f32[2,64,256]{2,1,0:T(8,128)S(1)}, f32[2,256]{1,0:T(2,128)S(1)}, f32[2,256,64]{1,2,0:T(8,128)S(1)}, f32[2,64]{1,0:T(2,128)S(1)}, /...) while((s32[]{:T(128)}, f32[2,64,256]{2,1,0:T(8,128)S(1)}, ...), condition=%wide.region_17.18_spmd, body=%wide.region_12.17_spmd.sunk | while | flops 127755136 | bytes 2386049 | solution.py:90
  149.2 0.4 convolution_subtract_fusion.42
  151.9 0.4 convolution_subtract_fusion.42
  154.6 0.4 convolution_subtract_fusion.42
  155.9 2.1 collective-permute-start.2
  158.0 9.8 %collective-permute-done.2 = f32[2,33088]{1,0:T(2,128)S(1)} collective-permute-done((f32[2,33088]{1,0:T(2,128)S(1)}, f32[2,33088]{1,0:T(2,128)S(1)}, u32[]{:S(2)}, u32[]{:S(2)}) %collective-permute-start.2) | collective-permute-done | bytes 264736 | tf_op jit(solution)/shard_map/state_hop/ppermute | solution.py:16
  168.2 10.8 %while.133 = (s32[]{:T(128)}, f32[2,64,256]{2,1,0:T(8,128)S(1)}, f32[2,256]{1,0:T(2,128)S(1)}, f32[2,256,64]{1,2,0:T(8,128)S(1)}, f32[2,64]{1,0:T(2,128)S(1)}, /...) while((s32[]{:T(128)}, f32[2,64,256]{2,1,0:T(8,128)S(1)}, ...), condition=%wide.region_23.24_spmd, body=%wide.region_18.23_spmd.sunk | while | flops 127755136 | bytes 2386049 | solution.py:90
  172.8 0.4 convolution_subtract_fusion.44
  175.5 0.4 convolution_subtract_fusion.44
  178.2 0.4 convolution_subtract_fusion.44
  179.6 1.9 collective-permute-start.3
  181.5 10.0 %collective-permute-done.3 = f32[2,33088]{1,0:T(2,128)S(1)} collective-permute-done((f32[2,33088]{1,0:T(2,128)S(1)}, f32[2,33088]{1,0:T(2,128)S(1)}, u32[]{:S(2)}, u32[]{:S(2)}) %collective-permute-start.3) | collective-permute-done | bytes 264736 | tf_op jit(solution)/shard_map/state_hop/ppermute | solution.py:16
  191.9 10.8 %while.134 = (s32[]{:T(128)}, f32[2,64,256]{2,1,0:T(8,128)S(1)}, f32[2,256]{1,0:T(2,128)S(1)}, f32[2,256,64]{1,2,0:T(8,128)S(1)}, f32[2,64]{1,0:T(2,128)S(1)}, /...) while((s32[]{:T(128)}, f32[2,64,256]{2,1,0:T(8,128)S(1)}, ...), condition=%wide.region_29.30_spmd, body=%wide.region_24.29_spmd.sunk | while | flops 127755136 | bytes 2386049 | solution.py:90
  196.5 0.4 convolution_subtract_fusion.46
  203.3 1.9 collective-permute-start.4
  205.2 10.0 %collective-permute-done.4 = f32[2,33088]{1,0:T(2,128)S(1)} collective-permute-done((f32[2,33088]{1,0:T(2,128)S(1)}, f32[2,33088]{1,0:T(2,128)S(1)}, u32[]{:S(2)}, u32[]{:S(2)}) %collective-permute-start.4) | collective-permute-done | bytes 264736 | tf_op jit(solution)/shard_map/state_hop/ppermute | solution.py:16
  215.6 10.8 %while.135 = (s32[]{:T(128)}, f32[2,64,256]{2,1,0:T(8,128)S(1)}, f32[2,256]{1,0:T(2,128)S(1)}, f32[2,256,64]{1,2,0:T(8,128)S(1)}, f32[2,64]{1,0:T(2,128)S(1)}, /...) while((s32[]{:T(128)}, f32[2,64,256]{2,1,0:T(8,128)S(1)}, ...), condition=%wide.region_35.36_spmd, body=%wide.region_30.35_spmd.sunk | while | flops 127755136 | bytes 2386049 | solution.py:90
  226.9 1.9 collective-permute-start.5
  228.9 10.0 %collective-permute-done.5 = f32[2,33088]{1,0:T(2,128)S(1)} collective-permute-done((f32[2,33088]{1,0:T(2,128)S(1)}, f32[2,33088]{1,0:T(2,128)S(1)}, u32[]{:S(2)}, u32[]{:S(2)}) %collective-permute-start.5) | collective-permute-done | bytes 264736 | tf_op jit(solution)/shard_map/state_hop/ppermute | solution.py:16
  239.3 10.8 %while.136 = (s32[]{:T(128)}, f32[2,64,256]{2,1,0:T(8,128)S(1)}, f32[2,256]{1,0:T(2,128)S(1)}, f32[2,256,64]{1,2,0:T(8,128)S(1)}, f32[2,64]{1,0:T(2,128)S(1)}, /...) while((s32[]{:T(128)}, f32[2,64,256]{2,1,0:T(8,128)S(1)}, ...), condition=%wide.region_41.42_spmd, body=%wide.region_36.41_spmd.sunk | while | flops 127755136 | bytes 2386049 | solution.py:90
  250.6 2.1 collective-permute-start.6
  253.1 9.4 %collective-permute-done.6 = f32[2,33088]{1,0:T(2,128)S(1)} collective-permute-done((f32[2,33088]{1,0:T(2,128)S(1)}, f32[2,33088]{1,0:T(2,128)S(1)}, u32[]{:S(2)}, u32[]{:S(2)}) %collective-permute-start.6) | collective-permute-done | bytes 264736 | tf_op jit(solution)/shard_map/state_hop/ppermute | solution.py:16
  263.0 20.7 %while.137 = (s32[]{:T(128)}, f32[2,64,256]{2,1,0:T(8,128)S(1)}, f32[2,256]{1,0:T(2,128)S(1)}, f32[2,256,64]{1,2,0:T(8,128)S(1)}, f32[2,64]{1,0:T(2,128)S(1)}, /...) while((s32[]{:T(128)}, f32[2,64,256]{2,1,0:T(8,128)S(1)}, ...), condition=%wide.region_49.50_spmd, body=%wide.region_42.49_spmd.sunk | while | flops 273236992 | bytes 4856473 | solution.py:90
  283.8 0.8 reshape.543
  284.6 3.3 all-to-all-start.1
  287.9 0.6 dynamic-slice
  288.5 3.5 all-to-all-done.1
  292.1 1.8 convolution_bitcast_fusion
  294.1 0.9 copy.289
  295.0 63.4 %all-reduce.2 = bf16[8,49152]{1,0:T(8,128)(2,1)S(1)} all-reduce(f32[8,49152]{1,0:T(8,128)S(1)} %bitcast.724), channel_id=2, replica_groups=mesh['seq'=8,'xlo'=2,'z'=8,'core'=2] {'z'}, use_global_device_ids=true, to_apply=%region_50.51.clone | all-reduce | flops 393216 | bytes 2359296
  358.4 0.8 constant_dynamic-slice_fusion.1
  359.2 0.6 convert_reduce_fusion
  359.7 0.7 convert_element_type.25
  (671 shorter events, 97.4 us)
Async XLA Ops:
  9.5 82.3 %all-to-all-start = ((bf16[32,2,8,3072]{3,2,1,0:T(8,128)(2,1)}), bf16[32,2,8,3072]{3,2,1,0:T(8,128)(2,1)S(1)}, u32[]{:S(2)}, u32[]{:S(2)}) async-start(bf16[32,2,8,3072]{3,2,1,0:T(8,128)(2,1)} %stack.2), calls=%async_computation | async-start | bytes 6291456 | tf_op jit(solution)/shard_map/all_to_all | solution.py:135
  19.0 273.1 %all-gather.2.cloned.1.call-start = ((), (), s32[]{:S(2)}) async-start(), calls=%async_computation.2 | async-start | bytes 1966080 | tf_op jit(solution)/shard_map/all_gather | solution.py:144
  19.7 72.3 %copy-start.7 = (bf16[1,3072]{1,0:T(2,128)(2,1)S(1)}, bf16[1,3072]{1,0:T(2,128)(2,1)}, u32[]{:S(2)}) copy-start(bf16[1,3072]{1,0:T(2,128)(2,1)} %param.29) | copy-start | bytes 18436
  91.8 1.3 copy-start.6
  94.2 0.9 copy-start
  94.2 0.9 copy-start.4
  94.2 0.9 copy-start.5
  94.2 0.9 copy-start.3
  94.3 0.9 copy-start.1
  94.3 0.9 copy-start.2
  106.5 13.4 %collective-permute-start = (f32[2,33088]{1,0:T(2,128)S(1)}, f32[2,33088]{1,0:T(2,128)S(1)}, u32[]{:S(2)}, u32[]{:S(2)}) collective-permute-start(f32[2,33088]{1,0:T(2,128)S(1)} %pad_maximum_fusion), channel_id=1, source_target_pairs={{0,32},{32,64},{64,96},{96,128},{128,160},{160,192},{192,224},{1,3... | collective-permute-start | bytes 794120 | tf_op jit(solution)/shard_map/state_hop/ppermute | solution.py:16
  131.7 12.5 %collective-permute-start.1 = (f32[2,33088]{1,0:T(2,128)S(1)}, f32[2,33088]{1,0:T(2,128)S(1)}, u32[]{:S(2)}, u32[]{:S(2)}) collective-permute-start(f32[2,33088]{1,0:T(2,128)S(1)} %pad_maximum_fusion.1), channel_id=1, source_target_pairs={{0,32},{32,64},{64,96},{96,128},{128,160},{160,192},{192,224},{1,3... | collective-permute-start | bytes 794120 | tf_op jit(solution)/shard_map/state_hop/ppermute | solution.py:16
  155.9 11.9 %collective-permute-start.2 = (f32[2,33088]{1,0:T(2,128)S(1)}, f32[2,33088]{1,0:T(2,128)S(1)}, u32[]{:S(2)}, u32[]{:S(2)}) collective-permute-start(f32[2,33088]{1,0:T(2,128)S(1)} %pad_maximum_fusion.2), channel_id=1, source_target_pairs={{0,32},{32,64},{64,96},{96,128},{128,160},{160,192},{192,224},{1,3... | collective-permute-start | bytes 794120 | tf_op jit(solution)/shard_map/state_hop/ppermute | solution.py:16
  179.6 11.9 %collective-permute-start.3 = (f32[2,33088]{1,0:T(2,128)S(1)}, f32[2,33088]{1,0:T(2,128)S(1)}, u32[]{:S(2)}, u32[]{:S(2)}) collective-permute-start(f32[2,33088]{1,0:T(2,128)S(1)} %pad_maximum_fusion.3), channel_id=1, source_target_pairs={{0,32},{32,64},{64,96},{96,128},{128,160},{160,192},{192,224},{1,3... | collective-permute-start | bytes 794120 | tf_op jit(solution)/shard_map/state_hop/ppermute | solution.py:16
  203.3 11.9 %collective-permute-start.4 = (f32[2,33088]{1,0:T(2,128)S(1)}, f32[2,33088]{1,0:T(2,128)S(1)}, u32[]{:S(2)}, u32[]{:S(2)}) collective-permute-start(f32[2,33088]{1,0:T(2,128)S(1)} %pad_maximum_fusion.4), channel_id=1, source_target_pairs={{0,32},{32,64},{64,96},{96,128},{128,160},{160,192},{192,224},{1,3... | collective-permute-start | bytes 794120 | tf_op jit(solution)/shard_map/state_hop/ppermute | solution.py:16
  226.9 11.9 %collective-permute-start.5 = (f32[2,33088]{1,0:T(2,128)S(1)}, f32[2,33088]{1,0:T(2,128)S(1)}, u32[]{:S(2)}, u32[]{:S(2)}) collective-permute-start(f32[2,33088]{1,0:T(2,128)S(1)} %pad_maximum_fusion.5), channel_id=1, source_target_pairs={{0,32},{32,64},{64,96},{96,128},{128,160},{160,192},{192,224},{1,3... | collective-permute-start | bytes 794120 | tf_op jit(solution)/shard_map/state_hop/ppermute | solution.py:16
  250.6 11.9 %collective-permute-start.6 = (f32[2,33088]{1,0:T(2,128)S(1)}, f32[2,33088]{1,0:T(2,128)S(1)}, u32[]{:S(2)}, u32[]{:S(2)}) collective-permute-start(f32[2,33088]{1,0:T(2,128)S(1)} %pad_maximum_fusion.6), channel_id=1, source_target_pairs={{0,32},{32,64},{64,96},{96,128},{128,160},{160,192},{192,224},{1,3... | collective-permute-start | bytes 794120 | tf_op jit(solution)/shard_map/state_hop/ppermute | solution.py:16
  263.0 24.9 %copy-start.8 = (u32[256]{0:T(256)S(1)}, u32[256]{0:T(256)}, u32[]{:S(2)}) copy-start(u32[256]{0:T(256)} %constant.275) | copy-start | bytes 3076
  284.6 7.4 %all-to-all-start.1 = ((bf16[4,2,4096]{2,1,0:T(2,128)(2,1)}), bf16[4,2,4096]{2,1,0:T(2,128)(2,1)S(1)}, u32[]{:S(2)}, u32[]{:S(2)}) async-start(bf16[4,2,4096]{2,1,0:T(2,128)(2,1)} %reshape.543), calls=%async_computation.1 | async-start | bytes 131072 | tf_op jit(solution)/shard_map/output_mix/all_to_all | solution.py:181
Sparse Core Ops, SparseCore 0:
  253.2 26.6 all-gather.1
